TPU v7x, 32 devices: a whole 2x2x4 slice. The times are simulated.
32 devices in a mesh: copies: 2 (over x), expert: 4 (over y, core), tm: 4 (over z).
Axes of the slice: x: 2, y: 2, z: 4, core: 2. Of those that a mesh axis runs over, the one named last changes fastest.
Arguments:
- tokens: bfloat16 [4, 1024, 2048], P('tm', ('copies', 'expert')), parts along dimension 1, may hold values from -6 to 6
- route_ids: int32 [4, 1024, 6], P('tm', ('copies', 'expert')), parts along dimension 1, may hold values from 0 to 15, all different within a row; in each aligned block of 128 rows (0 to 127, 128 to 255, ..., all dimensions but the last counted through in order) at most 72 rows name the same one
- route_probs: float32 [4, 1024, 6], P('tm', ('copies', 'expert')), parts along dimension 1, may hold values from 0.05 to 1
- step_size: float32 [8], P(('copies', 'tm')), parts along dimension 0, may hold values from 0.2 to 0.6
- start_state: float32 [1024, 2048], P(('copies', 'expert')), parts along dimension 0, may hold values from -6 to 6
- w_gate: bfloat16 [16, 2048, 768], P('expert'), may hold values from -0.125 to 0.125
- w_up: bfloat16 [16, 2048, 768], P('expert'), may hold values from -0.125 to 0.125
- w_down: bfloat16 [16, 768, 2048], P('expert'), may hold values from -0.21875 to 0.21875
Outputs:
- new_iterate: float32 [4, 1024, 2048], P('tm', ('copies', 'expert')), parts along dimension 1
There are 2 independent parts, one for each index of `copies`. A program takes and returns all parts, laid end to end along the dimension named above; an argument that names none is the same for every part. Nothing has to cross between parts.
Inputs may be any that keep to these rules, and one draw needn't show every extreme that they name: `route_ids`: each row names 6 different experts. In each aligned block of 128 rows (the tokens of one device), no expert is named by more than 72 rows, a bound that some block reaches.
All inputs are finite; a program needn't handle non-finite values.
Results may differ from a plain program's by a relative error of at most 0.0018.
Values may be sent and summed in bfloat16 or wider, within the bound.
A program may use at most 128 MiB of HBM per device.

v0:
```python
import jax
import jax.numpy as jnp
from jax import lax
from jax.sharding import PartitionSpec as P


def expert_rows(received, w_gate, w_up, w_down):
    local_count, source_count, slot_count, feature_count = received.shape
    flat_rows = received.reshape(local_count, source_count * slot_count, feature_count)
    gate_act = jnp.einsum("jrd,jdf->jrf", flat_rows, w_gate, preferred_element_type=jnp.float32)
    up_act = jnp.einsum("jrd,jdf->jrf", flat_rows, w_up, preferred_element_type=jnp.float32)
    hidden = (jax.nn.silu(gate_act) * up_act).astype(jnp.bfloat16)
    result = jnp.einsum("jrf,jfd->jrd", hidden, w_down, preferred_element_type=jnp.float32)
    return result.astype(jnp.bfloat16).reshape(local_count, source_count, slot_count, feature_count)


def shards(tokens, route_ids, route_probs, step_size, start_state, w_gate, w_up, w_down):
    tok_count = tokens.shape[1]
    feature_count = tokens.shape[2]
    topk_count = route_ids.shape[2]
    expert_total = w_gate.shape[0] * lax.axis_size("expert")
    capacity = 3 * tok_count * topk_count // (2 * expert_total)
    values = tokens[0].astype(jnp.float32)
    normed = (values * lax.rsqrt(jnp.mean(values * values, axis=-1, keepdims=True) + 1e-06)).astype(
        jnp.bfloat16
    )
    flat_ids = route_ids[0].reshape(-1)
    one_hot = (flat_ids[:, None] == jnp.arange(expert_total, dtype=jnp.int32)[None, :]).astype(
        jnp.int32
    )
    earlier = jnp.cumsum(one_hot, axis=0) - one_hot
    position = jnp.sum(earlier * one_hot, axis=1)
    slot_index = flat_ids * capacity + position
    slot_grid = slot_index[:, None] == jnp.arange(expert_total * capacity, dtype=jnp.int32)[None, :]
    dispatch_map = jnp.any(slot_grid.reshape(tok_count, topk_count, -1), axis=1).astype(
        jnp.bfloat16
    )
    packed = jnp.einsum(
        "ts,td->sd", dispatch_map, normed, preferred_element_type=jnp.float32
    ).astype(jnp.bfloat16)
    outgoing = packed.reshape(expert_total, 1, capacity, feature_count)
    received = lax.all_to_all(outgoing, "expert", split_axis=0, concat_axis=1, tiled=True)
    answered = expert_rows(received, w_gate, w_up, w_down)
    returned = lax.all_to_all(answered, "expert", split_axis=1, concat_axis=0, tiled=True)
    gathered = returned.reshape(expert_total * capacity, feature_count)[slot_index]
    gathered = gathered.reshape(tok_count, topk_count, feature_count).astype(jnp.float32)
    gate_probs = route_probs[0]
    weights = gate_probs / jnp.sum(gate_probs, axis=-1, keepdims=True)
    drift_rows = jnp.einsum("tk,tkd->td", weights, gathered, precision=lax.Precision.HIGHEST)
    increment = step_size[0] * drift_rows
    own_index = lax.axis_index("tm")
    shard_rows = lax.all_gather(
        increment[None].astype(jnp.bfloat16), "tm", axis=0, tiled=True
    ).astype(jnp.float32)
    below_own = jnp.arange(shard_rows.shape[0], dtype=jnp.int32) <= own_index
    summed = jnp.zeros_like(increment) + jnp.sum(
        jnp.where(below_own[:, None, None], shard_rows, 0.0), axis=0
    )
    return (start_state + summed)[None]


def solution(mesh):
    return jax.shard_map(
        shards,
        mesh=mesh,
        in_specs=(
            P("tm", ("copies", "expert"), None),
            P("tm", ("copies", "expert"), None),
            P("tm", ("copies", "expert"), None),
            P(("copies", "tm")),
            P(("copies", "expert"), None),
            P("expert", None, None),
            P("expert", None, None),
            P("expert", None, None),
        ),
        out_specs=P("tm", ("copies", "expert"), None),
        check_vma=False,
    )
```

profile of v0, /device:TPU:0, one launch (start us, length us, event | category | flops | bytes accessed | tf_op | source)
XLA Modules:
  0.0 237.0 jit_solution(10654996169284588786)
XLA Ops:
  6.5 0.8 copy.25
  7.6 1.7 reduce-window.6
  9.3 0.3 slice_reduce_fusion
  9.9 0.6 fusion.1
  10.5 1.2 fusion.3
  11.8 2.7 %convolution_convert_fusion = bf16[1152,2048]{1,0:T(8,128)(2,1)S(1)} fusion(pred[128,1152]{1,0:T(8,128)(4,1)S(1)} %fusion.1, bf16[1,128,2048]{2,1,0:T(8,128)(2,1)} %param.8, f32[128]{0:T(128)S(1)} %add_rsqrt_fusion), kind=kOutput, calls=%fused_computation.1 | convolution fusion | flops 607125504 | bytes 5390848 | tf_op jit(solution)/shard_map/ts,td->sd/dot_general | solution.py:38
  14.5 58.1 %all_to_all.30 = bf16[16,1,72,2048]{3,2,1,0:T(8,128)(2,1)S(1)} all-to-all(bf16[16,1,72,2048]{3,2,1,0:T(8,128)(2,1)S(1)} %bitcast.66), channel_id=1, replica_groups=mesh['copies'=2,'expert'=4,'tm'=4] {'expert'}, dimensions={0} | all-to-all | bytes 9437184 | tf_op jit(solution)/shard_map/all_to_all | solution.py:42
  72.5 0.7 copy.31
  73.3 2.2 copy-done
  75.5 0.6 slice-done.2
  76.0 5.7 %fusion.16 = f32[4,288,768]{2,1,0:T(8,128)} fusion(bf16[4,288,2048]{2,1,0:T(8,128)(2,1)S(1)} %bitcast.68, bf16[4,2048,768]{2,1,0:T(8,128)(2,1)S(1)} %bitcast.74), kind=kOutput, calls=%fused_computation.37 | convolution fusion | flops 3623878656 | bytes 20840448 | tf_op jit(solution)/shard_map/jrd,jdf->jrf/dot_general | solution.py:10
  81.7 15.9 %convolution_convert_fusion.1 = bf16[4,288,2048]{2,1,0:T(8,128)(2,1)} fusion(bf16[4,768,2048]{2,1,0:T(8,128)(2,1)} %param.15, f32[4,288,768]{2,1,0:T(8,128)} %fusion.16, bf16[4,288,2048]{2,1,0:T(8,128)(2,1)} %bitcast.69, bf16[4,2048,768]{2,1,0:T(8,128)(2,1)} %param.14), kind=kOutput, calls=%fused_computation.4 | convolution fusion | flops 7255425024 | bytes 38141952 | tf_op jit(solution)/shard_map/jrf,jfd->jrd/dot_general | solution.py:13
  97.6 5.2 %copy.32 = bf16[4,4,72,2048]{3,2,0,1:T(8,128)(2,1)} copy(bf16[4,4,72,2048]{3,2,1,0:T(8,128)(2,1)} %bitcast.70) | data formatting | bytes 9437184 | tf_op jit(solution)/shard_map/reshape | solution.py:14
  102.8 5.1 %all-to-all-start.1 = ((bf16[4,4,72,2048]{3,2,0,1:T(8,128)(2,1)}), bf16[4,4,72,2048]{3,2,0,1:T(8,128)(2,1)}, u32[]{:S(2)}, u32[]{:S(2)}) async-start(bf16[4,4,72,2048]{3,2,0,1:T(8,128)(2,1)} %copy.32), calls=%async_computation.1 | async-start | bytes 9437184 | tf_op jit(solution)/shard_map/all_to_all | solution.py:44
  107.9 0.2 all-gather.3.cloned.1.call-start
  108.1 0.1 mul.59
  109.1 52.6 %all-to-all-done.1 = bf16[4,4,72,2048]{3,2,0,1:T(8,128)(2,1)} async-done(((bf16[4,4,72,2048]{3,2,0,1:T(8,128)(2,1)}), bf16[4,4,72,2048]{3,2,0,1:T(8,128)(2,1)}, u32[]{:S(2)}, u32[]{:S(2)}) %all-to-all-start.1) | async-done | bytes 4718624 | tf_op jit(solution)/shard_map/all_to_all | solution.py:44
  161.7 9.3 %gather_fusion = bf16[768,2048]{1,0:T(8,128)(2,1)S(1)} fusion(bf16[1152,2048]{1,0:T(8,128)(2,1)} %bitcast.15, s32[1024]{0:T(1024)S(1)} %pad_clamp_fusion), kind=kCustom, calls=%fused_computation | custom fusion | bytes 6294528 | tf_op jit(solution)/shard_map/gather | solution.py:45
  171.0 2.9 %reshape.100 = bf16[128,6,2048]{2,1,0:T(8,128)(2,1)} reshape(bf16[768,2048]{1,0:T(8,128)(2,1)S(1)} %gather_fusion) | data formatting | bytes 6291456 | tf_op jit(solution)/shard_map/reshape | solution.py:46
  173.8 5.7 %fusion.17 = f32[128,1,2048]{2,1,0:T(1,128)S(1)} fusion(f32[128,6,1]{1,2,0:T(1,128)S(1)} %copy.33, bf16[128,6,2048]{2,1,0:T(8,128)(2,1)} %reshape.100), kind=kOutput, calls=%fused_computation.38 | convolution fusion | flops 18874368 | bytes 4197376 | tf_op jit(solution)/shard_map/tk,tkd->td/dot_general | solution.py:49
  179.6 1.1 fusion.5
  180.7 46.1 %all-gather.3.cloned.1.call-done = bf16[512,2048]{1,0:T(8,128)(2,1)} async-done(((bf16[128,2048]{1,0:T(8,128)(2,1)}), bf16[512,2048]{1,0:T(8,128)(2,1)}) %all-gather.3.cloned.1.call-update) | async-done | bytes 2097168 | tf_op jit(solution)/shard_map/all_gather | solution.py:52
  226.8 2.2 fusion
  229.0 1.1 add_bitcast_fusion
  (28 shorter events, 0.8 us)
Async XLA Ops:
  11.8 63.7 %slice-start = ((s8[12582912]{0:T(1024)(128)(4,1)}), s8[4194304]{0:T(1024)(128)(4,1)S(1)}, s32[]{:S(2)}) async-start(s8[12582912]{0:T(1024)(128)(4,1)} %bitcast.73), calls=%async_computation.3 | async-start | bytes 8388608
  14.4 61.0 %slice-start.1 = ((s8[12582912]{0:T(1024)(128)(4,1)}), s8[4194304]{0:T(1024)(128)(4,1)S(1)}, s32[]{:S(2)}) async-start(s8[12582912]{0:T(1024)(128)(4,1)} %bitcast.73), calls=%async_computation.4 | async-start | bytes 8388608
  72.5 3.5 %slice-start.2 = ((s8[12582912]{0:T(1024)(128)(4,1)}), s8[4194304]{0:T(1024)(128)(4,1)S(1)}, s32[]{:S(2)}) async-start(s8[12582912]{0:T(1024)(128)(4,1)} %bitcast.73), calls=%async_computation.5 | async-start | bytes 8388608
  73.3 2.2 copy-start
  102.8 5.5 %copy-start.2 = (f32[1,128,6]{1,0,2:T(1,128)S(1)}, f32[1,128,6]{1,0,2:T(1,128)}, u32[]{:S(2)}) copy-start(f32[1,128,6]{1,0,2:T(1,128)} %param.10) | copy-start | bytes 9220
  102.8 58.9 %all-to-all-start.1 = ((bf16[4,4,72,2048]{3,2,0,1:T(8,128)(2,1)}), bf16[4,4,72,2048]{3,2,0,1:T(8,128)(2,1)}, u32[]{:S(2)}, u32[]{:S(2)}) async-start(bf16[4,4,72,2048]{3,2,0,1:T(8,128)(2,1)} %copy.32), calls=%async_computation.1 | async-start | bytes 9437184 | tf_op jit(solution)/shard_map/all_to_all | solution.py:44
  107.9 118.9 %all-gather.3.cloned.1.call-start = ((), (), s32[]{:S(2)}) async-start(), calls=%async_computation.2 | async-start | bytes 2621440 | tf_op jit(solution)/shard_map/all_gather | solution.py:52
  173.8 55.2 %copy-start.1 = (f32[128,2048]{1,0:T(8,128)S(1)}, f32[128,2048]{1,0:T(8,128)}, u32[]{:S(2)}) copy-start(f32[128,2048]{1,0:T(8,128)} %param.12) | copy-start | bytes 3145732
Sparse Core Ops, SparseCore 0:
  180.8 45.9 all-gather.2
where the time goes:
time: 237 us
  waiting for transfers between devices  98.7 us (42%)
  blocking collectives  58.1 us (25%)
  matrix products  29.9 us (13%)
  local copies, waits for them, and re-layouts  22.6 us (10%)
  between operations  14.2 us (6%)
  other arithmetic  8.19 us (3%)
  starting transfers between devices  5.28 us (2%)
    all_to_all x1, blocking collectives, shards(): lax.all_to_all(outgoing, 'expert', split_axis=0, concat_axis=1, tiled=True)  58.1 us
    all_to_all x1, waiting for transfers between devices, shards(): lax.all_to_all(answered, 'expert', split_axis=1, concat_axis=0, tiled=True)  52.6 us
    all_gather x1, waiting for transfers between devices, shards(): lax.all_gather(increment[None].astype(jnp.bfloat16), 'tm', axis=0, tiled=...  46.1 us
    dot_general x1, matrix products, expert_rows(): jnp.einsum('jrf,jfd->jrd', hidden, w_down, preferred_element_type=jnp.flo...  15.9 us
    gather x1, local copies, waits for them, and re-layouts, shards(): returned.reshape(expert_total * capacity, feature_count)[slot_index]  9.28 us
    dot_general x1, matrix products, shards(): jnp.einsum('tk,tkd->td', weights, gathered, precision=lax.Precision.HIGHEST)  5.74 us
    dot_general x1, matrix products, expert_rows(): jnp.einsum('jrd,jdf->jrf', flat_rows, w_gate, preferred_element_type=jnp....  5.66 us
    reshape x1, local copies, waits for them, and re-layouts, expert_rows(): result.astype(jnp.bfloat16)  5.23 us
  transfers between devices with their start and end apart: 2, of which 2 were waited for; matrix products, arithmetic and copies ran while one was open for 0% of the time, Pallas kernels for 0%

commit v1 on v0

--- a/solution.py
+++ b/solution.py
@@ -41,7 +41,19 @@
     outgoing = packed.reshape(expert_total, 1, capacity, feature_count)
     received = lax.all_to_all(outgoing, "expert", split_axis=0, concat_axis=1, tiled=True)
     answered = expert_rows(received, w_gate, w_up, w_down)
-    returned = lax.all_to_all(answered, "expert", split_axis=1, concat_axis=0, tiled=True)
+    ways, here = (lax.axis_size("expert"), lax.axis_index("expert"))
+    width = answered.shape[1] // ways
+    shape = list(answered.shape)
+    shape[1] = width
+    height = shape[0]
+    shape[0] = height * ways
+    full = jnp.zeros(shape, answered.dtype)
+    for mask in range(ways):
+        part = lax.dynamic_slice_in_dim(answered, (here ^ mask) * width, width, axis=1)
+        if mask:
+            part = lax.ppermute(part, "expert", [(d, d ^ mask) for d in range(ways)])
+        full = lax.dynamic_update_slice_in_dim(full, part, (here ^ mask) * height, axis=0)
+    returned = full
     gathered = returned.reshape(expert_total * capacity, feature_count)[slot_index]
     gathered = gathered.reshape(tok_count, topk_count, feature_count).astype(jnp.float32)
     gate_probs = route_probs[0]

time: 237 us -> 241 us (1.017)
  blocking collectives: 58.1 us -> 0 us
  waiting for transfers between devices: 98.7 us -> 144 us
  local copies, waits for them, and re-layouts: 22.6 us -> 31.6 us
  matrix products: 29.9 us -> 34.9 us
    all_to_all x1 -> x0, blocking collectives: 58.1 us -> none  [shards(): lax.all_to_all(outgoing, 'expert', split_axis=0, concat_axis=1, tiled=True)]
    ppermute x0 -> x3, waiting for transfers between devices: none -> 43.2 us  [shards(): part = lax.ppermute(part, 'expert', [(d, d ^ mask) for d in range(ways)])]
    dynamic_update_slice x0 -> x4, local copies, waits for them, and re-layouts: none -> 5.88 us  [shards(): lax.dynamic_update_slice_in_dim(full, part, (here ^ mask) * height, axis=0)]
    reshape x1 -> x0, local copies, waits for them, and re-layouts: 5.23 us -> none  [expert_rows(): result.astype(jnp.bfloat16)]
    dynamic_slice x0 -> x1, local copies, waits for them, and re-layouts: none -> 3.9 us  [shards(): lax.dynamic_slice_in_dim(answered, (here ^ mask) * width, width, axis=1)]
    dot_general x1, matrix products: 5.66 us -> 8.58 us  [expert_rows(): jnp.einsum('jrd,jdf->jrf', flat_rows, w_gate, preferred_element_type=jnp....]
    broadcast_in_dim x0 -> x1, local copies, waits for them, and re-layouts: none -> 2.76 us  [shards(): full = jnp.zeros(shape, answered.dtype)]
  transfers between devices with their start and end apart: 2 -> 5, of which waited for: 2 -> 4; matrix products, arithmetic and copies ran while one was open for 0% -> 3% of each run, Pallas kernels for 0% -> 0%
where the time goes in v1:
time: 241 us; the launch traced here: 240 us
  waiting for transfers between devices  144 us (60%)
  matrix products  34.9 us (14%)
  local copies, waits for them, and re-layouts  31.6 us (13%)
  between operations  14.3 us (6%)
  other arithmetic  8.19 us (3%)
  starting transfers between devices  7.13 us (3%)
    all_to_all x1, waiting for transfers between devices, shards(): lax.all_to_all(outgoing, 'expert', split_axis=0, concat_axis=1, tiled=True)  54.2 us
    all_gather x1, waiting for transfers between devices, shards(): lax.all_gather(increment[None].astype(jnp.bfloat16), 'tm', axis=0, tiled=...  46.9 us
    ppermute x3, waiting for transfers between devices, shards(): part = lax.ppermute(part, 'expert', [(d, d ^ mask) for d in range(ways)])  43.2 us
    dot_general x1, matrix products, expert_rows(): jnp.einsum('jrf,jfd->jrd', hidden, w_down, preferred_element_type=jnp.flo...  15.9 us
    gather x1, local copies, waits for them, and re-layouts, shards(): returned.reshape(expert_total * capacity, feature_count)[slot_index]  9.28 us
    dot_general x1, matrix products, expert_rows(): jnp.einsum('jrd,jdf->jrf', flat_rows, w_gate, preferred_element_type=jnp....  8.58 us
    dynamic_update_slice x4, local copies, waits for them, and re-layouts, shards(): lax.dynamic_update_slice_in_dim(full, part, (here ^ mask) * height, axis=0)  5.88 us
    dot_general x1, matrix products, shards(): jnp.einsum('tk,tkd->td', weights, gathered, precision=lax.Precision.HIGHEST)  5.74 us
  transfers between devices with their start and end apart: 5, of which 4 were waited for; matrix products, arithmetic and copies ran while one was open for 3% of the time, Pallas kernels for 0%

profile of v1, /device:TPU:0, one launch (start us, length us, event | category | flops | bytes accessed | tf_op | source)
XLA Modules:
  0.0 240.5 jit_solution(17294049575246311470)
XLA Ops:
  7.6 1.7 reduce-window.6
  10.5 1.2 fusion.3
  11.8 4.7 %convolution_convert_fusion = bf16[1152,2048]{1,0:T(8,128)(2,1)} fusion(pred[128,1152]{1,0:T(8,128)(4,1)S(1)} %fusion.1, bf16[1,128,2048]{2,1,0:T(8,128)(2,1)} %param.8, f32[128]{0:T(128)S(1)} %add_rsqrt_fusion), kind=kOutput, calls=%fused_computation.1 | convolution fusion | flops 607125504 | bytes 5390848 | tf_op jit(solution)/shard_map/ts,td->sd/dot_general | solution.py:38
  16.5 4.9 %all-to-all-start = ((bf16[16,1,72,2048]{3,2,1,0:T(8,128)(2,1)}), bf16[16,1,72,2048]{3,2,1,0:T(8,128)(2,1)}, u32[]{:S(2)}, u32[]{:S(2)}) async-start(bf16[16,1,72,2048]{3,2,1,0:T(8,128)(2,1)} %bitcast.70), calls=%async_computation | async-start | bytes 9437184 | tf_op jit(solution)/shard_map/all_to_all | solution.py:42
  21.7 54.2 %all-to-all-done = bf16[16,1,72,2048]{3,2,1,0:T(8,128)(2,1)} async-done(((bf16[16,1,72,2048]{3,2,1,0:T(8,128)(2,1)}), bf16[16,1,72,2048]{3,2,1,0:T(8,128)(2,1)}, u32[]{:S(2)}, u32[]{:S(2)}) %all-to-all-start) | async-done | bytes 4718624 | tf_op jit(solution)/shard_map/all_to_all | solution.py:42
  75.9 3.0 %copy.40 = bf16[4,4,1,72,2048]{4,3,0,1,2:T(8,128)(2,1)S(1)} copy(bf16[4,4,1,72,2048]{4,3,1,0,2:T(8,128)(2,1)} %bitcast.8) | data formatting | bytes 9437184 | tf_op jit(solution)/shard_map/all_to_all | solution.py:42
  79.0 2.2 copy-done
  81.1 8.6 %fusion.16 = f32[4,288,768]{2,1,0:T(8,128)} fusion(bf16[4,288,2048]{2,1,0:T(8,128)(2,1)S(1)} %bitcast.71, bf16[4,2048,768]{2,1,0:T(8,128)(2,1)} %param.13), kind=kOutput, calls=%fused_computation.44 | convolution fusion | flops 3623878656 | bytes 20840448 | tf_op jit(solution)/shard_map/jrd,jdf->jrf/dot_general | solution.py:10
  89.7 15.9 %convolution_convert_fusion.1 = bf16[4,288,2048]{2,1,0:T(8,128)(2,1)} fusion(bf16[4,768,2048]{2,1,0:T(8,128)(2,1)} %param.15, f32[4,288,768]{2,1,0:T(8,128)} %fusion.16, bf16[4,288,2048]{2,1,0:T(8,128)(2,1)} %bitcast.72, bf16[4,2048,768]{2,1,0:T(8,128)(2,1)} %param.14), kind=kOutput, calls=%fused_computation.4 | convolution fusion | flops 7255425024 | bytes 38141952 | tf_op jit(solution)/shard_map/jrf,jfd->jrd/dot_general | solution.py:13
  105.6 3.9 %constant_dynamic-slice_fusion = (bf16[4,1,72,2048]{3,2,1,0:T(8,128)(2,1)}, bf16[4,1,72,2048]{3,2,1,0:T(8,128)(2,1)}, bf16[4,1,72,2048]{3,2,1,0:T(8,128)(2,1)}) fusion(bf16[4,4,72,2048]{3,2,1,0:T(8,128)(2,1)} %bitcast.73, s32[]{:T(128)S(6)} %select_n.44, s32[]{:T(128)S(6)} %select_n.42, s32[]{:T(128)S(6)} %select_n.40), kind=kLoop, calls=%fused_computation.38 | loop fusion | bytes 7077900 | tf_op jit(solution)/shard_map/dynamic_slice | solution.py:52
  110.6 1.9 collective-permute-start.2
  112.5 2.8 %broadcast_in_dim.17 = bf16[16,1,72,2048]{3,2,0,1:T(8,128)(2,1)} broadcast(bf16[]{:T(256)} %constant.18.clone.1), dimensions={} | broadcast | bytes 4718594 | tf_op jit(solution)/shard_map/broadcast_in_dim | solution.py:50
  115.2 2.5 %bitcast_dynamic-update-slice_fusion.3 = bf16[16,1,72,2048]{3,2,0,1:T(8,128)(2,1)} fusion(bf16[16,1,72,2048]{3,2,0,1:T(8,128)(2,1)} %broadcast_in_dim.17, s32[]{:T(128)S(6)} %select_n.39, bf16[4,4,72,2048]{3,2,1,0:T(8,128)(2,1)} %bitcast.74, s32[]{:T(128)S(6)} %select_n.38), kind=kLoop, calls=%fused_computation.14 | loop fusion | bytes 2359304 | tf_op jit(solution)/shard_map/dynamic_update_slice | solution.py:55
  117.7 1.1 bitcast_dynamic-update-slice_fusion.2
  118.8 20.0 %collective-permute-done.1 = bf16[4,1,72,2048]{3,2,1,0:T(8,128)(2,1)S(1)} collective-permute-done((bf16[4,1,72,2048]{3,2,1,0:T(8,128)(2,1)}, bf16[4,1,72,2048]{3,2,1,0:T(8,128)(2,1)S(1)}, u32[]{:S(2)}, u32[]{:S(2)}) %collective-permute-start.1) | collective-permute-done | bytes 1179680 | tf_op jit(solution)/shard_map/ppermute | solution.py:54
  139.9 23.3 %collective-permute-done.2 = bf16[4,1,72,2048]{3,2,1,0:T(8,128)(2,1)S(1)} collective-permute-done((bf16[4,1,72,2048]{3,2,1,0:T(8,128)(2,1)}, bf16[4,1,72,2048]{3,2,1,0:T(8,128)(2,1)S(1)}, u32[]{:S(2)}, u32[]{:S(2)}) %collective-permute-start.2) | collective-permute-done | bytes 1179680 | tf_op jit(solution)/shard_map/ppermute | solution.py:54
  163.1 1.2 bitcast_dynamic-update-slice_fusion
  164.4 9.3 %gather_fusion = bf16[768,2048]{1,0:T(8,128)(2,1)S(1)} fusion(bf16[1152,2048]{1,0:T(8,128)(2,1)} %bitcast.17, s32[1024]{0:T(1024)S(1)} %pad_clamp_fusion), kind=kCustom, calls=%fused_computation | custom fusion | bytes 6294528 | tf_op jit(solution)/shard_map/gather | solution.py:57
  173.7 2.9 %reshape.99 = bf16[128,6,2048]{2,1,0:T(8,128)(2,1)} reshape(bf16[768,2048]{1,0:T(8,128)(2,1)S(1)} %gather_fusion) | data formatting | bytes 6291456 | tf_op jit(solution)/shard_map/reshape | solution.py:58
  176.5 5.7 %fusion.17 = f32[128,1,2048]{2,1,0:T(1,128)S(1)} fusion(f32[128,6,1]{1,2,0:T(1,128)S(1)} %copy.45, bf16[128,6,2048]{2,1,0:T(8,128)(2,1)} %reshape.99), kind=kOutput, calls=%fused_computation.45 | convolution fusion | flops 18874368 | bytes 4197376 | tf_op jit(solution)/shard_map/tk,tkd->td/dot_general | solution.py:61
  182.3 1.1 fusion.5
  183.4 46.9 %all-gather.3.cloned.1.call-done = bf16[512,2048]{1,0:T(8,128)(2,1)} async-done(((bf16[128,2048]{1,0:T(8,128)(2,1)}), bf16[512,2048]{1,0:T(8,128)(2,1)}) %all-gather.3.cloned.1.call-update) | async-done | bytes 2097168 | tf_op jit(solution)/shard_map/all_gather | solution.py:64
  230.3 2.2 fusion
  232.5 1.1 add_bitcast_fusion
  (31 shorter events, 4.0 us)
Async XLA Ops:
  16.5 59.4 %all-to-all-start = ((bf16[16,1,72,2048]{3,2,1,0:T(8,128)(2,1)}), bf16[16,1,72,2048]{3,2,1,0:T(8,128)(2,1)}, u32[]{:S(2)}, u32[]{:S(2)}) async-start(bf16[16,1,72,2048]{3,2,1,0:T(8,128)(2,1)} %bitcast.70), calls=%async_computation | async-start | bytes 9437184 | tf_op jit(solution)/shard_map/all_to_all | solution.py:42
  21.4 208.9 %all-gather.3.cloned.1.call-start = ((), (), s32[]{:S(2)}) async-start(), calls=%async_computation.1 | async-start | bytes 2621440 | tf_op jit(solution)/shard_map/all_gather | solution.py:64
  78.9 2.2 copy-start
  105.6 4.1 %copy-start.2 = (f32[1,128,6]{1,0,2:T(1,128)S(1)}, f32[1,128,6]{1,0,2:T(1,128)}, u32[]{:S(2)}) copy-start(f32[1,128,6]{1,0,2:T(1,128)} %param.10) | copy-start | bytes 9220
  109.5 8.2 %collective-permute-start = (bf16[4,1,72,2048]{3,2,1,0:T(8,128)(2,1)}, bf16[4,1,72,2048]{3,2,1,0:T(8,128)(2,1)S(1)}, u32[]{:S(2)}, u32[]{:S(2)}) collective-permute-start(bf16[4,1,72,2048]{3,2,1,0:T(8,128)(2,1)} %get-tuple-element.7), channel_id=1, source_target_pairs={{0,4},{4,0},{8,12},{12,8},{1,5},{5,1},{9,13},{13,9},{2,6},{6,2},{1... | collective-permute-start | bytes 3538952 | tf_op jit(solution)/shard_map/ppermute | solution.py:54
  109.7 29.1 %collective-permute-start.1 = (bf16[4,1,72,2048]{3,2,1,0:T(8,128)(2,1)}, bf16[4,1,72,2048]{3,2,1,0:T(8,128)(2,1)S(1)}, u32[]{:S(2)}, u32[]{:S(2)}) collective-permute-start(bf16[4,1,72,2048]{3,2,1,0:T(8,128)(2,1)} %get-tuple-element.6), channel_id=1, source_target_pairs={{0,8},{4,12},{8,0},{12,4},{1,9},{5,13},{9,1},{13,5},{2,10},{6,14},... | collective-permute-start | bytes 3538952 | tf_op jit(solution)/shard_map/ppermute | solution.py:54
  110.6 52.6 %collective-permute-start.2 = (bf16[4,1,72,2048]{3,2,1,0:T(8,128)(2,1)}, bf16[4,1,72,2048]{3,2,1,0:T(8,128)(2,1)S(1)}, u32[]{:S(2)}, u32[]{:S(2)}) collective-permute-start(bf16[4,1,72,2048]{3,2,1,0:T(8,128)(2,1)} %get-tuple-element.5), channel_id=1, source_target_pairs={{0,12},{4,8},{8,4},{12,0},{1,13},{5,9},{9,5},{13,1},{2,14},{6,10},... | collective-permute-start | bytes 3538952 | tf_op jit(solution)/shard_map/ppermute | solution.py:54
  176.5 56.0 %copy-start.1 = (f32[128,2048]{1,0:T(8,128)S(1)}, f32[128,2048]{1,0:T(8,128)}, u32[]{:S(2)}) copy-start(f32[128,2048]{1,0:T(8,128)} %param.12) | copy-start | bytes 3145732
Sparse Core Ops, SparseCore 0:
  183.5 46.7 all-gather.2
